TPU v7x, 256 devices: a whole 4x4x8 slice. The times are simulated.
256 devices in a mesh: slab: 64 (over z, y, core), quad: 4 (over x).
Axes of the slice: x: 4, y: 4, z: 8, core: 2. Of those that a mesh axis runs over, the one named last changes fastest.
Arguments:
- grain_cell: int32 [4, 2097152], P(None, ('slab', 'quad')), may hold values from 0 to 254, as said below
- grain_count: int32 [256], P(('slab', 'quad')), may hold values from 2048 to 8192, as said below
- grain_weight: float32 [2097152], P(('slab', 'quad')), may hold values from 0.05 to 0.95
- grain_volume: float32 [2097152], P(('slab', 'quad')), may hold values from 0.02 to 0.4
- grain_velocity: float32 [3, 2097152], P(None, ('slab', 'quad')), may hold values from -6 to 6
Outputs:
- pressure: float32 [256, 64, 256], P('slab', 'quad')
- drag: float32 [3, 2097152], P(None, ('slab', 'quad'))
Inputs may be any that keep to these rules, and one draw needn't show every extreme that they name: grain_cell[0] < 4, grain_cell[1] < 4, grain_cell[2] < 16, grain_cell[3] <= 254; among the slots of one device at most 4096 name the same quarter, and on every device exactly 4096 name one quarter. `grain_count`: some device has all 8192 slots occupied.
All inputs are finite; a program needn't handle non-finite values.
Results may differ from a plain program's by a relative error of at most 0.00002.
Values sent between devices are 32-bit elements; how exact they have to be, the bound alone decides.
A program may use at most 128 MiB of HBM per device.

v0:
```python
import jax
import jax.numpy as jnp
from jax import lax
from jax.sharding import PartitionSpec as P

CH = 4
CA = 16
CB = 256
ITERS = 12
damping = 0.05
source_gain = 4.0


def extended(block, sides, width):
    for axis, dim in sides:
        count = lax.axis_size(axis)
        forward = [(i, i + 1) for i in range(count - 1)]
        backward = [(target, source) for source, target in forward]
        low = lax.ppermute(
            lax.slice_in_dim(block, block.shape[dim] - width, None, axis=dim), axis, forward
        )
        high = lax.ppermute(lax.slice_in_dim(block, 0, width, axis=dim), axis, backward)
        block = jnp.concatenate([low, block, high], axis=dim)
    return block


def neighbours(padded):
    centre = padded[1:-1, 1:-1]
    along = jnp.pad(centre, ((0, 0), (0, 0), (1, 1)))
    total = padded[2:, 1:-1] + padded[:-2, 1:-1] + padded[1:-1, 2:] + padded[1:-1, :-2]
    return total + along[:, :, 2:] + along[:, :, :-2]


def gradient(wide):
    vel_height = -0.5 * (wide[2:, 1:-1, 1:-1] - wide[:-2, 1:-1, 1:-1])
    vel_across = -0.5 * (wide[1:-1, 2:, 1:-1] - wide[1:-1, :-2, 1:-1])
    vel_along = -0.5 * (wide[1:-1, 1:-1, 2:] - wide[1:-1, 1:-1, :-2])
    return (vel_height, vel_across, vel_along)


def body(grain_cell, grain_count, grain_weight, grain_volume, grain_velocity):
    quarters = lax.axis_size("quad")
    layers, across_cells, along_cells = (CH, CA, CB)
    block = layers * across_cells * along_cells
    slots = jnp.arange(grain_weight.shape[0], dtype=jnp.int32)
    valid = (slots < grain_count[0]).astype(jnp.float32)
    mass = valid * grain_volume
    upper = 1.0 - grain_weight
    target = (
        (grain_cell[0] * layers + grain_cell[1]) * across_cells + grain_cell[2]
    ) * along_cells + grain_cell[3]
    amounts = jnp.stack([mass, mass * grain_velocity[0]])
    partial_value = jnp.zeros((2, quarters * block), jnp.float32)
    partial_value = (
        partial_value.at[:, target]
        .add(amounts * grain_weight)
        .at[:, target + 1]
        .add(amounts * upper)
    )
    partial_value = partial_value.reshape(2, quarters * layers, across_cells, along_cells)
    field = lax.psum_scatter(partial_value, "quad", scatter_dimension=1, tiled=True)
    solid = field[0]
    voidage = 1.0 / (1.0 + solid)
    source = source_gain * field[1]
    start = jnp.zeros((layers, across_cells, along_cells), jnp.float32)

    def relax(repeat, pressure):
        padded = extended(pressure, (("slab", 0), ("quad", 1)), 1)
        return (source + voidage * neighbours(padded)) / (6.0 * voidage + damping)

    pressure = lax.fori_loop(0, ITERS, relax, start)
    rimmed_p = extended(pressure, (("slab", 0), ("quad", 1)), 1)
    vel_height, vel_across, vel_along = gradient(jnp.pad(rimmed_p, ((0, 0), (0, 0), (1, 1))))
    stacked = jnp.stack([vel_height, vel_across, vel_along, solid])
    table = lax.all_gather(stacked, "quad", axis=2, tiled=True)
    across_all = across_cells * quarters
    table = table.reshape(4, layers * across_all * along_cells)
    source_index = (
        grain_cell[1] * across_all + grain_cell[0] * across_cells + grain_cell[2]
    ) * along_cells + grain_cell[3]
    sampled = grain_weight * table[:, source_index] + upper * table[:, source_index + 1]
    factor = mass * (1.0 + sampled[3]) ** 2
    drag = factor * (sampled[:3] - grain_velocity)
    return (pressure, drag)


def solution(mesh):
    placed = (
        P(None, ("slab", "quad")),
        P(("slab", "quad")),
        P(("slab", "quad")),
        P(("slab", "quad")),
        P(None, ("slab", "quad")),
    )
    return jax.shard_map(
        body,
        mesh=mesh,
        in_specs=placed,
        out_specs=(P("slab", "quad", None), P(None, ("slab", "quad"))),
        check_vma=False,
    )
```

profile of v0, /device:TPU:8, one launch (start us, length us, event | category | flops | bytes accessed | tf_op | source)
XLA Modules:
  0.0 598.2 jit_solution(5532912857880428166)
XLA Ops:
  12.5 2.7 copy.19
  15.2 2.7 copy.20
  18.0 57.5 %scatter_custom_fusion = f32[2,65536]{0,1:T(8,128)} fusion(s32[8192]{0:T(1024)S(1)} %bitcast.61, f32[8192,2]{1,0:T(8,128)} %copy.19, f32[]{:T(128)} %constant.44.clone.1), kind=kCustom, calls=%fused_computation.26 | custom fusion | flops 16384 | bytes 524800 | tf_op jit(solution)/shard_map/scatter-add | solution.py:56
  75.5 61.4 %scatter_fusion = f32[2,65536]{0,1:T(8,128)} fusion(f32[2,65536]{0,1:T(8,128)} %scatter_custom_fusion, s32[8192]{0:T(1024)S(1)} %bitcast.58, f32[8192,2]{1,0:T(8,128)} %copy.20), kind=kCustom, calls=%fused_computation.3 | custom fusion | flops 16384 | bytes 229376 | tf_op jit(solution)/shard_map/scatter-add | solution.py:58
  136.9 20.1 %copy.21 = f32[2,16,16,256]{3,2,1,0:T(8,128)} copy(f32[2,16,16,256]{0,3,2,1:T(8,128)} %bitcast.51) | data formatting | bytes 1048576 | tf_op jit(solution)/shard_map/reshape | solution.py:60
  158.4 50.0 %all-reduce.5.cloned.1.call-done = f32[2,16,16,256]{3,2,1,0:T(8,128)} async-done(((f32[2,16,16,256]{3,2,1,0:T(8,128)}), f32[2,16,16,256]{3,2,1,0:T(8,128)}) %all-reduce.5.cloned.1.call-update) | async-done | bytes 524304
  209.3 178.4 %while.13 = (s32[]{:T(128)}, f32[4,16,256]{2,1,0:T(8,128)S(1)}, f32[4,16,256]{2,1,0:T(8,128)S(1)}, f32[4,16,256]{2,1,0:T(8,128)S(1)}, s32[]{:T(128)}, /*index=5*/s32[]{:T(128)}) while((s32[]{:T(128)}, f32[4,16,256]{2,1,0:T(8,128)S(1)}, f32[4,16,256]{2,1,0:T(8,128)S(1)}, f32[4,16,256]{2,1,0:T(8,128)S(1)}, s32[]{:T(128)}, ...), condition=%wide.region_4.5_spmd.clone, body=%wide.region_3.4_spmd.clone.sunk | while | flops 317443 | bytes 794863 | solution.py:71
  209.3 1.9 collective-permute-start
  211.3 2.4 collective-permute-start.1
  213.7 2.6 collective-permute-done.1
  216.3 2.4 collective-permute-start.2
  220.1 4.2 collective-permute-done.3
  226.4 2.4 collective-permute-start.1
  228.8 2.6 collective-permute-done.1
  231.4 3.6 collective-permute-start.2
  236.4 4.2 collective-permute-done.3
  242.6 2.4 collective-permute-start.1
  245.1 2.6 collective-permute-done.1
  247.7 2.9 collective-permute-start.2
  251.9 4.2 collective-permute-done.3
  258.2 2.4 collective-permute-start.1
  260.6 2.6 collective-permute-done.1
  266.5 4.2 collective-permute-done.3
  272.8 2.4 collective-permute-start.1
  275.2 2.6 collective-permute-done.1
  281.1 4.2 collective-permute-done.3
  285.5 1.9 collective-permute-start
  287.4 2.4 collective-permute-start.1
  289.8 2.6 collective-permute-done.1
  295.7 4.2 collective-permute-done.3
  302.0 2.4 collective-permute-start.1
  304.4 2.6 collective-permute-done.1
  307.1 1.9 collective-permute-start.2
  310.3 4.2 collective-permute-done.3
  316.6 2.4 collective-permute-start.1
  319.0 2.6 collective-permute-done.1
  325.0 4.2 collective-permute-done.3
  331.2 2.4 collective-permute-start.1
  333.7 2.6 collective-permute-done.1
  339.6 4.2 collective-permute-done.3
  343.9 1.9 collective-permute-start
  345.8 2.4 collective-permute-start.1
  348.3 2.6 collective-permute-done.1
  354.2 4.2 collective-permute-done.3
  360.5 2.4 collective-permute-start.1
  362.9 2.6 collective-permute-done.1
  368.8 4.2 collective-permute-done.3
  375.1 3.9 collective-permute-start.1
  383.4 4.2 collective-permute-done.3
  387.7 6.0 collective-permute-start.5
  393.7 1.9 collective-permute-start.4
  395.7 6.4 %collective-permute-done.4 = f32[1,16,256]{2,1,0:T(8,128)S(1)} collective-permute-done((f32[1,16,256]{2,1,0:T(8,128)S(1)}, f32[1,16,256]{2,1,0:T(8,128)S(1)}, u32[]{:S(2)}, u32[]{:S(2)}) %collective-permute-start.4) | collective-permute-done | bytes 16416 | tf_op jit(solution)/shard_map/ppermute | solution.py:22
  403.4 4.7 collective-permute-start.7
  410.4 62.0 %all-gather.2.cloned.1.call-done = f32[4,4,64,256]{3,2,1,0:T(8,128)} async-done(((f32[4,4,16,256]{3,2,1,0:T(8,128)}), f32[4,4,64,256]{3,2,1,0:T(8,128)}) %all-gather.2.cloned.1.call-update) | async-done | bytes 1048592 | tf_op jit(solution)/shard_map/all_gather | solution.py:75
  472.4 17.7 %copy.22 = f32[4,4,64,256]{0,3,2,1:T(8,128)} copy(f32[4,4,64,256]{3,2,1,0:T(8,128)} %all-gather.2.cloned.1.call-done) | data formatting | bytes 2097152 | tf_op jit(solution)/shard_map/all_gather | solution.py:75
  490.1 38.4 %gather_fusion = f32[8192,4]{1,0:T(8,128)} fusion(f32[4,65536]{0,1:T(8,128)} %bitcast.52, s32[8192]{0:T(1024)S(1)} %broadcast_clamp_fusion.1), kind=kCustom, calls=%fused_computation | custom fusion | bytes 294912 | tf_op jit(solution)/shard_map/gather | solution.py:81
  528.5 38.4 %gather_fusion.1 = f32[8192,4]{1,0:T(8,128)} fusion(f32[4,65536]{0,1:T(8,128)} %bitcast.53, s32[8192]{0:T(1024)S(1)} %broadcast_clamp_fusion), kind=kCustom, calls=%fused_computation.1 | custom fusion | bytes 294912 | tf_op jit(solution)/shard_map/gather | solution.py:81
  566.9 7.0 %add_bitcast_fusion = f32[4,8192]{0,1:T(8,128)S(1)} fusion(f32[8192,4]{1,0:T(8,128)} %gather_fusion.1, f32[8192,4]{1,0:T(8,128)} %gather_fusion, f32[8192]{0:T(1024)S(1)} %broadcast_subtract_fusion, f32[8192]{0:T(1024)S(1)} %copy-done.2), kind=kLoop, calls=%fused_computation.31 | loop fusion | flops 98304 | bytes 458752 | tf_op jit(solution)/shard_map/add | solution.py:81
  574.0 1.9 copy-done
  575.9 2.2 fusion.11
  578.2 2.8 copy.23
  581.1 2.6 copy.24
  583.7 4.2 broadcast_multiply_fusion
  587.9 3.5 copy.25
  (141 shorter events, 61.1 us)
Async XLA Ops:
  7.2 201.2 %all-reduce.5.cloned.1.call-start = ((), (), s32[]{:S(2)}) async-start(), calls=%async_computation.1 | async-start | bytes 1048576
  136.9 20.2 %copy-start.4 = (u32[256]{0:T(256)S(1)}, u32[256]{0:T(256)}, u32[]{:S(2)}) copy-start(u32[256]{0:T(256)} %constant.62) | copy-start | bytes 3076
  157.1 315.3 %all-gather.2.cloned.1.call-start = ((), (), s32[]{:S(2)}) async-start(), calls=%async_computation | async-start | bytes 1310720 | tf_op jit(solution)/shard_map/all_gather | solution.py:75
  209.3 4.3 collective-permute-start
  211.3 5.1 collective-permute-start.1
  216.3 3.7 collective-permute-start.2
  218.8 5.5 collective-permute-start.3
  224.4 4.3 collective-permute-start
  226.4 5.1 collective-permute-start.1
  231.4 4.9 collective-permute-start.2
  235.0 5.5 collective-permute-start.3
  240.7 4.3 collective-permute-start
  242.6 5.1 collective-permute-start.1
  247.7 4.2 collective-permute-start.2
  250.6 5.5 collective-permute-start.3
  256.3 4.3 collective-permute-start
  258.2 5.1 collective-permute-start.1
  263.3 3.3 collective-permute-start.2
  265.2 5.5 collective-permute-start.3
  270.9 4.3 collective-permute-start
  272.8 5.1 collective-permute-start.1
  277.9 3.3 collective-permute-start.2
  279.8 5.5 collective-permute-start.3
  285.5 4.3 collective-permute-start
  287.4 5.1 collective-permute-start.1
  292.5 3.3 collective-permute-start.2
  294.4 5.5 collective-permute-start.3
  300.1 4.3 collective-permute-start
  302.0 5.1 collective-permute-start.1
  307.1 3.3 collective-permute-start.2
  309.0 5.5 collective-permute-start.3
  314.7 4.3 collective-permute-start
  316.6 5.1 collective-permute-start.1
  321.7 3.3 collective-permute-start.2
  323.6 5.5 collective-permute-start.3
  329.3 4.3 collective-permute-start
  331.2 5.1 collective-permute-start.1
  336.3 3.3 collective-permute-start.2
  338.2 5.5 collective-permute-start.3
  343.9 4.3 collective-permute-start
  345.8 5.1 collective-permute-start.1
  350.9 3.3 collective-permute-start.2
  352.8 5.6 collective-permute-start.3
  358.6 4.3 collective-permute-start
  360.5 5.1 collective-permute-start.1
  365.6 3.2 collective-permute-start.2
  367.4 5.5 collective-permute-start.3
  373.1 5.8 collective-permute-start
  375.1 5.1 collective-permute-start.1
  380.1 3.3 collective-permute-start.2
  382.1 5.5 collective-permute-start.3
  387.7 102.4 %copy-start.1 = (f32[4,16,256]{2,1,0:T(8,128)}, f32[4,16,256]{2,1,0:T(8,128)S(1)}, u32[]{:S(2)}) copy-start(f32[4,16,256]{2,1,0:T(8,128)S(1)} %get-tuple-element.75) | copy-start | bytes 196612
  387.7 7.9 %collective-permute-start.5 = (f32[1,16,256]{2,1,0:T(8,128)S(1)}, f32[1,16,256]{2,1,0:T(8,128)S(1)}, u32[]{:S(2)}, u32[]{:S(2)}) collective-permute-start(f32[1,16,256]{2,1,0:T(8,128)S(1)} %get-tuple-element.105), channel_id=1, source_target_pairs={{0,4},{4,8},{8,12},{12,16},{16,20},{20,24},{24,28},{28,32},{32,36}... | collective-permute-start | bytes 49160 | tf_op jit(solution)/shard_map/ppermute | solution.py:19
  393.7 8.4 %collective-permute-start.4 = (f32[1,16,256]{2,1,0:T(8,128)S(1)}, f32[1,16,256]{2,1,0:T(8,128)S(1)}, u32[]{:S(2)}, u32[]{:S(2)}) collective-permute-start(f32[1,16,256]{2,1,0:T(8,128)S(1)} %get-tuple-element.104), channel_id=1, source_target_pairs={{4,0},{8,4},{12,8},{16,12},{20,16},{24,20},{28,24},{32,28},{36,32}... | collective-permute-start | bytes 49160 | tf_op jit(solution)/shard_map/ppermute | solution.py:22
  402.1 6.0 %collective-permute-start.6 = (f32[6,1,256]{2,1,0:T(1,128)S(1)}, f32[6,1,256]{2,1,0:T(1,128)S(1)}, u32[]{:S(2)}, u32[]{:S(2)}) collective-permute-start(f32[6,1,256]{2,1,0:T(1,128)S(1)} %get-tuple-element.101), channel_id=1, source_target_pairs={{1,0},{2,1},{3,2},{5,4},{6,5},{7,6},{9,8},{10,9},{11,10},{13,12},{... | collective-permute-start | bytes 18440 | tf_op jit(solution)/shard_map/ppermute | solution.py:22
  403.4 5.9 collective-permute-start.7
  410.4 156.5 %copy-start.2 = (f32[8192]{0:T(1024)S(1)}, f32[8192]{0:T(1024)}, u32[]{:S(2)}) copy-start(f32[8192]{0:T(1024)} %param.9) | copy-start | bytes 98308
  574.0 2.0 copy-start
  575.9 5.1 copy-start.3
Sparse Core Ops, SparseCore 0:
  157.2 51.1 all-reduce.4
  410.5 61.8 all-gather.1
where the time goes:
time: 601 us; the launch traced here: 598 us
  waiting for transfers between devices  200 us (33%)
  other arithmetic  140 us (23%)
  local copies, waits for them, and re-layouts  133 us (22%)
  starting transfers between devices  109 us (18%)
  between operations  15.6 us (3%)
    scatter-add x2, other arithmetic, body(): partial_value = partial_value.at[:, target].add(amounts * grain_weight).a...  119 us
    ppermute x26, starting transfers between devices, extended(): lax.ppermute(lax.slice_in_dim(block, block.shape[dim] - width, None, axis...  67.2 us
    all_gather x1, waiting for transfers between devices, body(): table = lax.all_gather(stacked, 'quad', axis=2, tiled=True)  62 us
    ppermute x26, waiting for transfers between devices, extended(): lax.ppermute(lax.slice_in_dim(block, 0, width, axis=dim), axis, backward)  56.8 us
    unnamed x3, waiting for transfers between devices  50 us
    ppermute x26, starting transfers between devices, extended(): lax.ppermute(lax.slice_in_dim(block, 0, width, axis=dim), axis, backward)  41.8 us
    gather x1, local copies, waits for them, and re-layouts, body(): table[:, source_index + 1]  38.4 us
    gather x1, local copies, waits for them, and re-layouts, body(): table[:, source_index]  38.4 us
  transfers between devices with their start and end apart: 54, of which 28 were waited for; matrix products, arithmetic and copies ran while one was open for 0% of the time, Pallas kernels for 0%

commit v1 on v0

--- a/solution.py
+++ b/solution.py
@@ -72,7 +72,10 @@
     rimmed_p = extended(pressure, (("slab", 0), ("quad", 1)), 1)
     vel_height, vel_across, vel_along = gradient(jnp.pad(rimmed_p, ((0, 0), (0, 0), (1, 1))))
     stacked = jnp.stack([vel_height, vel_across, vel_along, solid])
-    table = lax.all_gather(stacked, "quad", axis=2, tiled=True)
+    devices = lax.axis_size("quad")
+    parts = jnp.stack([stacked for _ in range(devices)])
+    parts = lax.all_to_all(parts, "quad", split_axis=0, concat_axis=0)
+    table = jnp.concatenate(parts, axis=2)
     across_all = across_cells * quarters
     table = table.reshape(4, layers * across_all * along_cells)
     source_index = (

time: 601 us -> 589 us (0.980)
  the two profiles are of different devices: /device:TPU:8 before, /device:TPU:121 now
where the time goes in v1:
time: 589 us; the launch traced here: 587 us
  starting transfers between devices  187 us (32%)
  other arithmetic  139 us (24%)
  local copies, waits for them, and re-layouts  132 us (22%)
  waiting for transfers between devices  112 us (19%)
  between operations  15.6 us (3%)
    ppermute x26, starting transfers between devices, extended(): lax.ppermute(lax.slice_in_dim(block, block.shape[dim] - width, None, axis...  137 us
    scatter-add x2, other arithmetic, body(): partial_value = partial_value.at[:, target].add(amounts * grain_weight).a...  119 us
    unnamed x2, waiting for transfers between devices  46.6 us
    ppermute x26, starting transfers between devices, extended(): lax.ppermute(lax.slice_in_dim(block, 0, width, axis=dim), axis, backward)  45.9 us
    ppermute x26, waiting for transfers between devices, extended(): lax.ppermute(lax.slice_in_dim(block, 0, width, axis=dim), axis, backward)  43.3 us
    gather x1, local copies, waits for them, and re-layouts, body(): table[:, source_index + 1]  38.3 us
    gather x1, local copies, waits for them, and re-layouts, body(): table[:, source_index]  38.3 us
    reshape x1, local copies, waits for them, and re-layouts, body(): partial_value.reshape(2, quarters * layers, across_cells, along_cells)  20.1 us
  transfers between devices with their start and end apart: 54, of which 28 were waited for; matrix products, arithmetic and copies ran while one was open for 0% of the time, Pallas kernels for 0%

profile of v1, /device:TPU:121, one launch (start us, length us, event | category | flops | bytes accessed | tf_op | source)
XLA Modules:
  0.0 586.9 jit_solution(3914998909556620562)
XLA Ops:
  12.5 2.7 copy.19
  15.2 2.7 copy.20
  18.0 57.5 %scatter_custom_fusion = f32[2,65536]{0,1:T(8,128)} fusion(s32[8192]{0:T(1024)S(1)} %bitcast.63, f32[8192,2]{1,0:T(8,128)} %copy.19, f32[]{:T(128)} %constant.44.clone.1), kind=kCustom, calls=%fused_computation.26 | custom fusion | flops 16384 | bytes 524800 | tf_op jit(solution)/shard_map/scatter-add | solution.py:56
  75.5 61.4 %scatter_fusion = f32[2,65536]{0,1:T(8,128)} fusion(f32[2,65536]{0,1:T(8,128)} %scatter_custom_fusion, s32[8192]{0:T(1024)S(1)} %bitcast.60, f32[8192,2]{1,0:T(8,128)} %copy.20), kind=kCustom, calls=%fused_computation.3 | custom fusion | flops 16384 | bytes 229376 | tf_op jit(solution)/shard_map/scatter-add | solution.py:58
  136.9 20.1 %copy.21 = f32[2,16,16,256]{3,2,1,0:T(8,128)} copy(f32[2,16,16,256]{0,3,2,1:T(8,128)} %bitcast.52) | data formatting | bytes 1048576 | tf_op jit(solution)/shard_map/reshape | solution.py:60
  158.4 46.6 %all-reduce.5.cloned.1.call-done = f32[2,16,16,256]{3,2,1,0:T(8,128)} async-done(((f32[2,16,16,256]{3,2,1,0:T(8,128)}), f32[2,16,16,256]{3,2,1,0:T(8,128)}) %all-reduce.5.cloned.1.call-update) | async-done | bytes 524304
  205.8 216.4 %while.13 = (s32[]{:T(128)}, f32[4,16,256]{2,1,0:T(8,128)S(1)}, f32[4,16,256]{2,1,0:T(8,128)S(1)}, f32[4,16,256]{2,1,0:T(8,128)S(1)}, s32[]{:T(128)}, /*index=5*/s32[]{:T(128)}) while((s32[]{:T(128)}, f32[4,16,256]{2,1,0:T(8,128)S(1)}, f32[4,16,256]{2,1,0:T(8,128)S(1)}, f32[4,16,256]{2,1,0:T(8,128)S(1)}, s32[]{:T(128)}, ...), condition=%wide.region_4.5_spmd.clone, body=%wide.region_3.4_spmd.clone.sunk | while | flops 317443 | bytes 794863 | solution.py:71
  205.9 4.8 collective-permute-start
  210.7 4.2 collective-permute-start.1
  215.7 2.2 collective-permute-start.2
  219.2 3.1 collective-permute-done.3
  222.5 3.2 collective-permute-start
  225.7 7.6 %collective-permute-start.1 = (f32[1,16,256]{2,1,0:T(8,128)S(1)}, f32[1,16,256]{2,1,0:T(8,128)S(1)}, u32[]{:S(2)}, u32[]{:S(2)}) collective-permute-start(f32[1,16,256]{2,1,0:T(8,128)S(1)} %get-tuple-element.140), channel_id=1, source_target_pairs={{0,4},{4,8},{8,12},{12,16},{16,20},{20,24},{24,28},{28,32},{32,36}... | collective-permute-start | bytes 49160 | tf_op jit(solution)/shard_map/while/body/eval_jaxpr/ppermute | solution.py:19
  234.2 3.4 collective-permute-start.2
  238.9 3.1 collective-permute-done.3
  242.1 1.9 collective-permute-start
  244.1 9.0 %collective-permute-start.1 = (f32[1,16,256]{2,1,0:T(8,128)S(1)}, f32[1,16,256]{2,1,0:T(8,128)S(1)}, u32[]{:S(2)}, u32[]{:S(2)}) collective-permute-start(f32[1,16,256]{2,1,0:T(8,128)S(1)} %get-tuple-element.140), channel_id=1, source_target_pairs={{0,4},{4,8},{8,12},{12,16},{16,20},{20,24},{24,28},{28,32},{32,36}... | collective-permute-start | bytes 49160 | tf_op jit(solution)/shard_map/while/body/eval_jaxpr/ppermute | solution.py:19
  253.9 2.4 collective-permute-start.2
  257.7 3.1 collective-permute-done.3
  260.9 1.9 collective-permute-start
  262.8 9.0 %collective-permute-start.1 = (f32[1,16,256]{2,1,0:T(8,128)S(1)}, f32[1,16,256]{2,1,0:T(8,128)S(1)}, u32[]{:S(2)}, u32[]{:S(2)}) collective-permute-start(f32[1,16,256]{2,1,0:T(8,128)S(1)} %get-tuple-element.140), channel_id=1, source_target_pairs={{0,4},{4,8},{8,12},{12,16},{16,20},{20,24},{24,28},{28,32},{32,36}... | collective-permute-start | bytes 49160 | tf_op jit(solution)/shard_map/while/body/eval_jaxpr/ppermute | solution.py:19
  275.6 3.1 collective-permute-done.3
  278.8 1.9 collective-permute-start
  280.7 9.0 %collective-permute-start.1 = (f32[1,16,256]{2,1,0:T(8,128)S(1)}, f32[1,16,256]{2,1,0:T(8,128)S(1)}, u32[]{:S(2)}, u32[]{:S(2)}) collective-permute-start(f32[1,16,256]{2,1,0:T(8,128)S(1)} %get-tuple-element.140), channel_id=1, source_target_pairs={{0,4},{4,8},{8,12},{12,16},{16,20},{20,24},{24,28},{28,32},{32,36}... | collective-permute-start | bytes 49160 | tf_op jit(solution)/shard_map/while/body/eval_jaxpr/ppermute | solution.py:19
  293.5 3.1 collective-permute-done.3
  296.7 1.9 collective-permute-start
  298.7 9.0 %collective-permute-start.1 = (f32[1,16,256]{2,1,0:T(8,128)S(1)}, f32[1,16,256]{2,1,0:T(8,128)S(1)}, u32[]{:S(2)}, u32[]{:S(2)}) collective-permute-start(f32[1,16,256]{2,1,0:T(8,128)S(1)} %get-tuple-element.140), channel_id=1, source_target_pairs={{0,4},{4,8},{8,12},{12,16},{16,20},{20,24},{24,28},{28,32},{32,36}... | collective-permute-start | bytes 49160 | tf_op jit(solution)/shard_map/while/body/eval_jaxpr/ppermute | solution.py:19
  311.4 3.1 collective-permute-done.3
  314.7 1.9 collective-permute-start
  316.6 9.0 %collective-permute-start.1 = (f32[1,16,256]{2,1,0:T(8,128)S(1)}, f32[1,16,256]{2,1,0:T(8,128)S(1)}, u32[]{:S(2)}, u32[]{:S(2)}) collective-permute-start(f32[1,16,256]{2,1,0:T(8,128)S(1)} %get-tuple-element.140), channel_id=1, source_target_pairs={{0,4},{4,8},{8,12},{12,16},{16,20},{20,24},{24,28},{28,32},{32,36}... | collective-permute-start | bytes 49160 | tf_op jit(solution)/shard_map/while/body/eval_jaxpr/ppermute | solution.py:19
  326.4 1.6 collective-permute-start.2
  329.4 3.1 collective-permute-done.3
  332.6 1.9 collective-permute-start
  334.5 9.0 %collective-permute-start.1 = (f32[1,16,256]{2,1,0:T(8,128)S(1)}, f32[1,16,256]{2,1,0:T(8,128)S(1)}, u32[]{:S(2)}, u32[]{:S(2)}) collective-permute-start(f32[1,16,256]{2,1,0:T(8,128)S(1)} %get-tuple-element.140), channel_id=1, source_target_pairs={{0,4},{4,8},{8,12},{12,16},{16,20},{20,24},{24,28},{28,32},{32,36}... | collective-permute-start | bytes 49160 | tf_op jit(solution)/shard_map/while/body/eval_jaxpr/ppermute | solution.py:19
  347.3 3.1 collective-permute-done.3
  350.5 1.9 collective-permute-start
  352.4 9.0 %collective-permute-start.1 = (f32[1,16,256]{2,1,0:T(8,128)S(1)}, f32[1,16,256]{2,1,0:T(8,128)S(1)}, u32[]{:S(2)}, u32[]{:S(2)}) collective-permute-start(f32[1,16,256]{2,1,0:T(8,128)S(1)} %get-tuple-element.140), channel_id=1, source_target_pairs={{0,4},{4,8},{8,12},{12,16},{16,20},{20,24},{24,28},{28,32},{32,36}... | collective-permute-start | bytes 49160 | tf_op jit(solution)/shard_map/while/body/eval_jaxpr/ppermute | solution.py:19
  365.2 3.1 collective-permute-done.3
  368.4 1.9 collective-permute-start
  370.4 9.0 %collective-permute-start.1 = (f32[1,16,256]{2,1,0:T(8,128)S(1)}, f32[1,16,256]{2,1,0:T(8,128)S(1)}, u32[]{:S(2)}, u32[]{:S(2)}) collective-permute-start(f32[1,16,256]{2,1,0:T(8,128)S(1)} %get-tuple-element.140), channel_id=1, source_target_pairs={{0,4},{4,8},{8,12},{12,16},{16,20},{20,24},{24,28},{28,32},{32,36}... | collective-permute-start | bytes 49160 | tf_op jit(solution)/shard_map/while/body/eval_jaxpr/ppermute | solution.py:19
  383.1 3.1 collective-permute-done.3
  386.4 1.9 collective-permute-start
  388.3 9.0 %collective-permute-start.1 = (f32[1,16,256]{2,1,0:T(8,128)S(1)}, f32[1,16,256]{2,1,0:T(8,128)S(1)}, u32[]{:S(2)}, u32[]{:S(2)}) collective-permute-start(f32[1,16,256]{2,1,0:T(8,128)S(1)} %get-tuple-element.140), channel_id=1, source_target_pairs={{0,4},{4,8},{8,12},{12,16},{16,20},{20,24},{24,28},{28,32},{32,36}... | collective-permute-start | bytes 49160 | tf_op jit(solution)/shard_map/while/body/eval_jaxpr/ppermute | solution.py:19
  398.1 1.6 collective-permute-start.2
  401.1 3.1 collective-permute-done.3
  404.3 1.9 collective-permute-start
  406.2 9.0 %collective-permute-start.1 = (f32[1,16,256]{2,1,0:T(8,128)S(1)}, f32[1,16,256]{2,1,0:T(8,128)S(1)}, u32[]{:S(2)}, u32[]{:S(2)}) collective-permute-start(f32[1,16,256]{2,1,0:T(8,128)S(1)} %get-tuple-element.140), channel_id=1, source_target_pairs={{0,4},{4,8},{8,12},{12,16},{16,20},{20,24},{24,28},{28,32},{32,36}... | collective-permute-start | bytes 49160 | tf_op jit(solution)/shard_map/while/body/eval_jaxpr/ppermute | solution.py:19
  419.0 3.1 collective-permute-done.3
  422.2 9.0 %collective-permute-start.5 = (f32[1,16,256]{2,1,0:T(8,128)S(1)}, f32[1,16,256]{2,1,0:T(8,128)S(1)}, u32[]{:S(2)}, u32[]{:S(2)}) collective-permute-start(f32[1,16,256]{2,1,0:T(8,128)S(1)} %get-tuple-element.105), channel_id=1, source_target_pairs={{0,4},{4,8},{8,12},{12,16},{16,20},{20,24},{24,28},{28,32},{32,36}... | collective-permute-start | bytes 49160 | tf_op jit(solution)/shard_map/ppermute | solution.py:19
  431.2 1.9 collective-permute-start.4
  433.1 6.4 %collective-permute-done.4 = f32[1,16,256]{2,1,0:T(8,128)S(1)} collective-permute-done((f32[1,16,256]{2,1,0:T(8,128)S(1)}, f32[1,16,256]{2,1,0:T(8,128)S(1)}, u32[]{:S(2)}, u32[]{:S(2)}) %collective-permute-start.4) | collective-permute-done | bytes 16416 | tf_op jit(solution)/shard_map/ppermute | solution.py:22
  440.9 4.0 collective-permute-start.7
  447.1 3.7 all-to-all-start
  450.8 11.5 %all-to-all-done = f32[4,4,4,16,256]{4,3,2,1,0:T(8,128)S(1)} async-done(((f32[4,4,4,16,256]{4,3,2,1,0:T(8,128)}), f32[4,4,4,16,256]{4,3,2,1,0:T(8,128)S(1)}, u32[]{:S(2)}, u32[]{:S(2)}) %all-to-all-start) | async-done | bytes 1048608 | tf_op jit(solution)/shard_map/all_to_all | solution.py:77
  462.4 16.6 %copy.22 = f32[4,4,4,16,256]{0,4,3,2,1:T(8,128)} copy(f32[4,4,4,16,256]{4,3,1,0,2:T(8,128)S(1)} %bitcast.56) | data formatting | bytes 2097152 | tf_op jit(solution)/shard_map/reshape | solution.py:78
  479.0 38.3 %gather_fusion = f32[8192,4]{1,0:T(8,128)} fusion(f32[4,65536]{0,1:T(8,128)} %bitcast.53, s32[8192]{0:T(1024)S(1)} %broadcast_clamp_fusion.1), kind=kCustom, calls=%fused_computation | custom fusion | bytes 294912 | tf_op jit(solution)/shard_map/gather | solution.py:84
  517.3 38.3 %gather_fusion.1 = f32[8192,4]{1,0:T(8,128)} fusion(f32[4,65536]{0,1:T(8,128)} %bitcast.54, s32[8192]{0:T(1024)S(1)} %broadcast_clamp_fusion), kind=kCustom, calls=%fused_computation.1 | custom fusion | bytes 294912 | tf_op jit(solution)/shard_map/gather | solution.py:84
  555.6 7.0 %add_bitcast_fusion = f32[4,8192]{0,1:T(8,128)S(1)} fusion(f32[8192,4]{1,0:T(8,128)} %gather_fusion.1, f32[8192,4]{1,0:T(8,128)} %gather_fusion, f32[8192]{0:T(1024)S(1)} %broadcast_subtract_fusion, f32[8192]{0:T(1024)S(1)} %copy-done.2), kind=kLoop, calls=%fused_computation.31 | loop fusion | flops 98304 | bytes 458752 | tf_op jit(solution)/shard_map/add | solution.py:84
  562.6 2.0 copy-done
  564.6 2.2 fusion.11
  566.8 2.8 copy.23
  569.7 2.7 copy.24
  572.4 4.2 broadcast_multiply_fusion
  576.6 3.5 copy.25
  (141 shorter events, 48.5 us)
Async XLA Ops:
  7.2 197.8 %all-reduce.5.cloned.1.call-start = ((), (), s32[]{:S(2)}) async-start(), calls=%async_computation.1 | async-start | bytes 1048576
  136.9 20.2 %copy-start.4 = (u32[256]{0:T(256)S(1)}, u32[256]{0:T(256)}, u32[]{:S(2)}) copy-start(u32[256]{0:T(256)} %constant.62) | copy-start | bytes 3076
  205.9 9.0 %collective-permute-start = (f32[1,16,256]{2,1,0:T(8,128)S(1)}, f32[1,16,256]{2,1,0:T(8,128)S(1)}, u32[]{:S(2)}, u32[]{:S(2)}) collective-permute-start(f32[1,16,256]{2,1,0:T(8,128)S(1)} %get-tuple-element.139), channel_id=1, source_target_pairs={{4,0},{8,4},{12,8},{16,12},{20,16},{24,20},{28,24},{32,28},{36,32}... | collective-permute-start | bytes 49160 | tf_op jit(solution)/shard_map/while/body/eval_jaxpr/ppermute | solution.py:22
  210.7 5.1 collective-permute-start.1
  215.7 3.5 collective-permute-start.2
  217.9 4.4 collective-permute-start.3
  222.5 10.9 %collective-permute-start = (f32[1,16,256]{2,1,0:T(8,128)S(1)}, f32[1,16,256]{2,1,0:T(8,128)S(1)}, u32[]{:S(2)}, u32[]{:S(2)}) collective-permute-start(f32[1,16,256]{2,1,0:T(8,128)S(1)} %get-tuple-element.139), channel_id=1, source_target_pairs={{4,0},{8,4},{12,8},{16,12},{20,16},{24,20},{28,24},{32,28},{36,32}... | collective-permute-start | bytes 49160 | tf_op jit(solution)/shard_map/while/body/eval_jaxpr/ppermute | solution.py:22
  225.7 8.5 %collective-permute-start.1 = (f32[1,16,256]{2,1,0:T(8,128)S(1)}, f32[1,16,256]{2,1,0:T(8,128)S(1)}, u32[]{:S(2)}, u32[]{:S(2)}) collective-permute-start(f32[1,16,256]{2,1,0:T(8,128)S(1)} %get-tuple-element.140), channel_id=1, source_target_pairs={{0,4},{4,8},{8,12},{12,16},{16,20},{20,24},{24,28},{28,32},{32,36}... | collective-permute-start | bytes 49160 | tf_op jit(solution)/shard_map/while/body/eval_jaxpr/ppermute | solution.py:19
  234.2 4.7 collective-permute-start.2
  237.6 4.4 collective-permute-start.3
  242.1 10.9 %collective-permute-start = (f32[1,16,256]{2,1,0:T(8,128)S(1)}, f32[1,16,256]{2,1,0:T(8,128)S(1)}, u32[]{:S(2)}, u32[]{:S(2)}) collective-permute-start(f32[1,16,256]{2,1,0:T(8,128)S(1)} %get-tuple-element.139), channel_id=1, source_target_pairs={{4,0},{8,4},{12,8},{16,12},{20,16},{24,20},{28,24},{32,28},{36,32}... | collective-permute-start | bytes 49160 | tf_op jit(solution)/shard_map/while/body/eval_jaxpr/ppermute | solution.py:22
  244.1 9.8 %collective-permute-start.1 = (f32[1,16,256]{2,1,0:T(8,128)S(1)}, f32[1,16,256]{2,1,0:T(8,128)S(1)}, u32[]{:S(2)}, u32[]{:S(2)}) collective-permute-start(f32[1,16,256]{2,1,0:T(8,128)S(1)} %get-tuple-element.140), channel_id=1, source_target_pairs={{0,4},{4,8},{8,12},{12,16},{16,20},{20,24},{24,28},{28,32},{32,36}... | collective-permute-start | bytes 49160 | tf_op jit(solution)/shard_map/while/body/eval_jaxpr/ppermute | solution.py:19
  253.9 3.8 collective-permute-start.2
  256.3 4.4 collective-permute-start.3
  260.9 10.9 %collective-permute-start = (f32[1,16,256]{2,1,0:T(8,128)S(1)}, f32[1,16,256]{2,1,0:T(8,128)S(1)}, u32[]{:S(2)}, u32[]{:S(2)}) collective-permute-start(f32[1,16,256]{2,1,0:T(8,128)S(1)} %get-tuple-element.139), channel_id=1, source_target_pairs={{4,0},{8,4},{12,8},{16,12},{20,16},{24,20},{28,24},{32,28},{36,32}... | collective-permute-start | bytes 49160 | tf_op jit(solution)/shard_map/while/body/eval_jaxpr/ppermute | solution.py:22
  262.8 9.8 %collective-permute-start.1 = (f32[1,16,256]{2,1,0:T(8,128)S(1)}, f32[1,16,256]{2,1,0:T(8,128)S(1)}, u32[]{:S(2)}, u32[]{:S(2)}) collective-permute-start(f32[1,16,256]{2,1,0:T(8,128)S(1)} %get-tuple-element.140), channel_id=1, source_target_pairs={{0,4},{4,8},{8,12},{12,16},{16,20},{20,24},{24,28},{28,32},{32,36}... | collective-permute-start | bytes 49160 | tf_op jit(solution)/shard_map/while/body/eval_jaxpr/ppermute | solution.py:19
  272.6 3.0 collective-permute-start.2
  274.3 4.4 collective-permute-start.3
  278.8 10.9 %collective-permute-start = (f32[1,16,256]{2,1,0:T(8,128)S(1)}, f32[1,16,256]{2,1,0:T(8,128)S(1)}, u32[]{:S(2)}, u32[]{:S(2)}) collective-permute-start(f32[1,16,256]{2,1,0:T(8,128)S(1)} %get-tuple-element.139), channel_id=1, source_target_pairs={{4,0},{8,4},{12,8},{16,12},{20,16},{24,20},{28,24},{32,28},{36,32}... | collective-permute-start | bytes 49160 | tf_op jit(solution)/shard_map/while/body/eval_jaxpr/ppermute | solution.py:22
  280.7 9.8 %collective-permute-start.1 = (f32[1,16,256]{2,1,0:T(8,128)S(1)}, f32[1,16,256]{2,1,0:T(8,128)S(1)}, u32[]{:S(2)}, u32[]{:S(2)}) collective-permute-start(f32[1,16,256]{2,1,0:T(8,128)S(1)} %get-tuple-element.140), channel_id=1, source_target_pairs={{0,4},{4,8},{8,12},{12,16},{16,20},{20,24},{24,28},{28,32},{32,36}... | collective-permute-start | bytes 49160 | tf_op jit(solution)/shard_map/while/body/eval_jaxpr/ppermute | solution.py:19
  290.5 3.0 collective-permute-start.2
  292.2 4.4 collective-permute-start.3
  296.7 10.9 %collective-permute-start = (f32[1,16,256]{2,1,0:T(8,128)S(1)}, f32[1,16,256]{2,1,0:T(8,128)S(1)}, u32[]{:S(2)}, u32[]{:S(2)}) collective-permute-start(f32[1,16,256]{2,1,0:T(8,128)S(1)} %get-tuple-element.139), channel_id=1, source_target_pairs={{4,0},{8,4},{12,8},{16,12},{20,16},{24,20},{28,24},{32,28},{36,32}... | collective-permute-start | bytes 49160 | tf_op jit(solution)/shard_map/while/body/eval_jaxpr/ppermute | solution.py:22
  298.7 9.8 %collective-permute-start.1 = (f32[1,16,256]{2,1,0:T(8,128)S(1)}, f32[1,16,256]{2,1,0:T(8,128)S(1)}, u32[]{:S(2)}, u32[]{:S(2)}) collective-permute-start(f32[1,16,256]{2,1,0:T(8,128)S(1)} %get-tuple-element.140), channel_id=1, source_target_pairs={{0,4},{4,8},{8,12},{12,16},{16,20},{20,24},{24,28},{28,32},{32,36}... | collective-permute-start | bytes 49160 | tf_op jit(solution)/shard_map/while/body/eval_jaxpr/ppermute | solution.py:19
  308.5 3.0 collective-permute-start.2
  310.1 4.4 collective-permute-start.3
  314.7 10.9 %collective-permute-start = (f32[1,16,256]{2,1,0:T(8,128)S(1)}, f32[1,16,256]{2,1,0:T(8,128)S(1)}, u32[]{:S(2)}, u32[]{:S(2)}) collective-permute-start(f32[1,16,256]{2,1,0:T(8,128)S(1)} %get-tuple-element.139), channel_id=1, source_target_pairs={{4,0},{8,4},{12,8},{16,12},{20,16},{24,20},{28,24},{32,28},{36,32}... | collective-permute-start | bytes 49160 | tf_op jit(solution)/shard_map/while/body/eval_jaxpr/ppermute | solution.py:22
  316.6 9.8 %collective-permute-start.1 = (f32[1,16,256]{2,1,0:T(8,128)S(1)}, f32[1,16,256]{2,1,0:T(8,128)S(1)}, u32[]{:S(2)}, u32[]{:S(2)}) collective-permute-start(f32[1,16,256]{2,1,0:T(8,128)S(1)} %get-tuple-element.140), channel_id=1, source_target_pairs={{0,4},{4,8},{8,12},{12,16},{16,20},{20,24},{24,28},{28,32},{32,36}... | collective-permute-start | bytes 49160 | tf_op jit(solution)/shard_map/while/body/eval_jaxpr/ppermute | solution.py:19
  326.4 3.0 collective-permute-start.2
  328.1 4.4 collective-permute-start.3
  332.6 10.9 %collective-permute-start = (f32[1,16,256]{2,1,0:T(8,128)S(1)}, f32[1,16,256]{2,1,0:T(8,128)S(1)}, u32[]{:S(2)}, u32[]{:S(2)}) collective-permute-start(f32[1,16,256]{2,1,0:T(8,128)S(1)} %get-tuple-element.139), channel_id=1, source_target_pairs={{4,0},{8,4},{12,8},{16,12},{20,16},{24,20},{28,24},{32,28},{36,32}... | collective-permute-start | bytes 49160 | tf_op jit(solution)/shard_map/while/body/eval_jaxpr/ppermute | solution.py:22
  334.5 9.8 %collective-permute-start.1 = (f32[1,16,256]{2,1,0:T(8,128)S(1)}, f32[1,16,256]{2,1,0:T(8,128)S(1)}, u32[]{:S(2)}, u32[]{:S(2)}) collective-permute-start(f32[1,16,256]{2,1,0:T(8,128)S(1)} %get-tuple-element.140), channel_id=1, source_target_pairs={{0,4},{4,8},{8,12},{12,16},{16,20},{20,24},{24,28},{28,32},{32,36}... | collective-permute-start | bytes 49160 | tf_op jit(solution)/shard_map/while/body/eval_jaxpr/ppermute | solution.py:19
  344.3 3.0 collective-permute-start.2
  346.0 4.4 collective-permute-start.3
  350.5 10.9 %collective-permute-start = (f32[1,16,256]{2,1,0:T(8,128)S(1)}, f32[1,16,256]{2,1,0:T(8,128)S(1)}, u32[]{:S(2)}, u32[]{:S(2)}) collective-permute-start(f32[1,16,256]{2,1,0:T(8,128)S(1)} %get-tuple-element.139), channel_id=1, source_target_pairs={{4,0},{8,4},{12,8},{16,12},{20,16},{24,20},{28,24},{32,28},{36,32}... | collective-permute-start | bytes 49160 | tf_op jit(solution)/shard_map/while/body/eval_jaxpr/ppermute | solution.py:22
  352.4 9.8 %collective-permute-start.1 = (f32[1,16,256]{2,1,0:T(8,128)S(1)}, f32[1,16,256]{2,1,0:T(8,128)S(1)}, u32[]{:S(2)}, u32[]{:S(2)}) collective-permute-start(f32[1,16,256]{2,1,0:T(8,128)S(1)} %get-tuple-element.140), channel_id=1, source_target_pairs={{0,4},{4,8},{8,12},{12,16},{16,20},{20,24},{24,28},{28,32},{32,36}... | collective-permute-start | bytes 49160 | tf_op jit(solution)/shard_map/while/body/eval_jaxpr/ppermute | solution.py:19
  362.3 3.0 collective-permute-start.2
  363.9 4.4 collective-permute-start.3
  368.4 10.9 %collective-permute-start = (f32[1,16,256]{2,1,0:T(8,128)S(1)}, f32[1,16,256]{2,1,0:T(8,128)S(1)}, u32[]{:S(2)}, u32[]{:S(2)}) collective-permute-start(f32[1,16,256]{2,1,0:T(8,128)S(1)} %get-tuple-element.139), channel_id=1, source_target_pairs={{4,0},{8,4},{12,8},{16,12},{20,16},{24,20},{28,24},{32,28},{36,32}... | collective-permute-start | bytes 49160 | tf_op jit(solution)/shard_map/while/body/eval_jaxpr/ppermute | solution.py:22
  370.4 9.8 %collective-permute-start.1 = (f32[1,16,256]{2,1,0:T(8,128)S(1)}, f32[1,16,256]{2,1,0:T(8,128)S(1)}, u32[]{:S(2)}, u32[]{:S(2)}) collective-permute-start(f32[1,16,256]{2,1,0:T(8,128)S(1)} %get-tuple-element.140), channel_id=1, source_target_pairs={{0,4},{4,8},{8,12},{12,16},{16,20},{20,24},{24,28},{28,32},{32,36}... | collective-permute-start | bytes 49160 | tf_op jit(solution)/shard_map/while/body/eval_jaxpr/ppermute | solution.py:19
  380.2 3.0 collective-permute-start.2
  381.8 4.4 collective-permute-start.3
  386.4 10.9 %collective-permute-start = (f32[1,16,256]{2,1,0:T(8,128)S(1)}, f32[1,16,256]{2,1,0:T(8,128)S(1)}, u32[]{:S(2)}, u32[]{:S(2)}) collective-permute-start(f32[1,16,256]{2,1,0:T(8,128)S(1)} %get-tuple-element.139), channel_id=1, source_target_pairs={{4,0},{8,4},{12,8},{16,12},{20,16},{24,20},{28,24},{32,28},{36,32}... | collective-permute-start | bytes 49160 | tf_op jit(solution)/shard_map/while/body/eval_jaxpr/ppermute | solution.py:22
  388.3 9.8 %collective-permute-start.1 = (f32[1,16,256]{2,1,0:T(8,128)S(1)}, f32[1,16,256]{2,1,0:T(8,128)S(1)}, u32[]{:S(2)}, u32[]{:S(2)}) collective-permute-start(f32[1,16,256]{2,1,0:T(8,128)S(1)} %get-tuple-element.140), channel_id=1, source_target_pairs={{0,4},{4,8},{8,12},{12,16},{16,20},{20,24},{24,28},{28,32},{32,36}... | collective-permute-start | bytes 49160 | tf_op jit(solution)/shard_map/while/body/eval_jaxpr/ppermute | solution.py:19
  398.1 3.0 collective-permute-start.2
  399.8 4.4 collective-permute-start.3
  404.3 10.9 %collective-permute-start = (f32[1,16,256]{2,1,0:T(8,128)S(1)}, f32[1,16,256]{2,1,0:T(8,128)S(1)}, u32[]{:S(2)}, u32[]{:S(2)}) collective-permute-start(f32[1,16,256]{2,1,0:T(8,128)S(1)} %get-tuple-element.139), channel_id=1, source_target_pairs={{4,0},{8,4},{12,8},{16,12},{20,16},{24,20},{28,24},{32,28},{36,32}... | collective-permute-start | bytes 49160 | tf_op jit(solution)/shard_map/while/body/eval_jaxpr/ppermute | solution.py:22
  406.2 9.8 %collective-permute-start.1 = (f32[1,16,256]{2,1,0:T(8,128)S(1)}, f32[1,16,256]{2,1,0:T(8,128)S(1)}, u32[]{:S(2)}, u32[]{:S(2)}) collective-permute-start(f32[1,16,256]{2,1,0:T(8,128)S(1)} %get-tuple-element.140), channel_id=1, source_target_pairs={{0,4},{4,8},{8,12},{12,16},{16,20},{20,24},{24,28},{28,32},{32,36}... | collective-permute-start | bytes 49160 | tf_op jit(solution)/shard_map/while/body/eval_jaxpr/ppermute | solution.py:19
  416.0 3.0 collective-permute-start.2
  417.7 4.4 collective-permute-start.3
  422.2 56.8 %copy-start.1 = (f32[4,16,256]{2,1,0:T(8,128)}, f32[4,16,256]{2,1,0:T(8,128)S(1)}, u32[]{:S(2)}) copy-start(f32[4,16,256]{2,1,0:T(8,128)S(1)} %get-tuple-element.75) | copy-start | bytes 196612
  422.2 10.9 %collective-permute-start.5 = (f32[1,16,256]{2,1,0:T(8,128)S(1)}, f32[1,16,256]{2,1,0:T(8,128)S(1)}, u32[]{:S(2)}, u32[]{:S(2)}) collective-permute-start(f32[1,16,256]{2,1,0:T(8,128)S(1)} %get-tuple-element.105), channel_id=1, source_target_pairs={{0,4},{4,8},{8,12},{12,16},{16,20},{20,24},{24,28},{28,32},{32,36}... | collective-permute-start | bytes 49160 | tf_op jit(solution)/shard_map/ppermute | solution.py:19
  431.2 8.4 %collective-permute-start.4 = (f32[1,16,256]{2,1,0:T(8,128)S(1)}, f32[1,16,256]{2,1,0:T(8,128)S(1)}, u32[]{:S(2)}, u32[]{:S(2)}) collective-permute-start(f32[1,16,256]{2,1,0:T(8,128)S(1)} %get-tuple-element.104), channel_id=1, source_target_pairs={{4,0},{8,4},{12,8},{16,12},{20,16},{24,20},{28,24},{32,28},{36,32}... | collective-permute-start | bytes 49160 | tf_op jit(solution)/shard_map/ppermute | solution.py:22
  439.6 5.3 collective-permute-start.6
  440.9 4.8 collective-permute-start.7
  447.1 15.3 %all-to-all-start = ((f32[4,4,4,16,256]{4,3,2,1,0:T(8,128)}), f32[4,4,4,16,256]{4,3,2,1,0:T(8,128)S(1)}, u32[]{:S(2)}, u32[]{:S(2)}) async-start(f32[4,4,4,16,256]{4,3,2,1,0:T(8,128)} %stack.35), calls=%async_computation | async-start | bytes 2097152 | tf_op jit(solution)/shard_map/all_to_all | solution.py:77
  462.4 93.2 %copy-start.2 = (f32[8192]{0:T(1024)S(1)}, f32[8192]{0:T(1024)}, u32[]{:S(2)}) copy-start(f32[8192]{0:T(1024)} %param.9) | copy-start | bytes 98308
  562.6 2.0 copy-start
  564.6 5.1 copy-start.3
Sparse Core Ops, SparseCore 0:
  157.2 47.6 all-reduce.4
